TPU v7x, 32 devices: a whole 2x2x4 slice. The times are simulated.
32 devices in a mesh: groups: 2 (over y), tm: 4 (over z), segment: 2 (over x), head: 2 (over core).
Axes of the slice: x: 2, y: 2, z: 4, core: 2. Of those that a mesh axis runs over, the one named last changes fastest.
Arguments:
- hidden_in: bfloat16 [768, 3072], P(('groups', 'tm'), 'head'), parts along dimension 0, may hold values from -6 to 6
- key_cache: bfloat16 [2, 768, 3072], P('segment', ('groups', 'tm'), 'head'), parts along dimension 1, may hold values from -6 to 6
- value_cache: bfloat16 [2, 768, 3072], P('segment', ('groups', 'tm'), 'head'), parts along dimension 1, may hold values from -6 to 6
- query_gain: float32 [2, 128], P('segment'), may hold values from 0.4 to 1.6
- key_gain: float32 [2, 128], P('segment'), may hold values from 0.4 to 1.6
- out_gate: float32 [2, 3072], P('segment', 'head'), may hold values from 0.5 to 2
- span_ids: int32 [768], P('groups'), parts along dimension 0, may hold values from 0 to 2, as said below
Outputs:
- layer_outputs: bfloat16 [2, 768, 3072], P('segment', ('groups', 'tm'), 'head'), parts along dimension 1
There are 2 independent parts, one for each index of `groups`. A program takes and returns all parts, laid end to end along the dimension named above; an argument that names none is the same for every part. Nothing has to cross between parts.
Inputs may be any that keep to these rules, and one draw needn't show every extreme that they name: span_ids never fall and rise by one from span to span; every span but the first and the last holds exactly 192 tokens, and the first and the last together hold 192, each at least one.
All inputs are finite; a program needn't handle non-finite values.
Results may differ from a plain program's by a relative error of at most 0.011.
Values may be sent and summed in bfloat16 or wider, within the bound.
No kernel may reach another device: no remote copies, remote signals or barrier semaphores. Data moves between devices by JAX's collectives and lax.ppermute only.
A program may use at most 64 MiB of HBM per device.

v0:
```python
import math
import jax
import jax.numpy as jnp
from jax import lax
from jax.sharding import PartitionSpec as P

HEAD_DIM = 128


def passed_along(shard, axis, by):
    devices = lax.axis_size(axis)
    pairs = [(i, i + by) for i in range(devices) if 0 <= i + by < devices]
    return lax.ppermute(shard, axis, pairs)


def head_normalize(features, gain_row):
    row_count = features.shape[0]
    shaped = features.astype(jnp.float32).reshape(row_count, -1, HEAD_DIM)
    inverse_rms = lax.rsqrt(jnp.mean(shaped * shaped, axis=-1, keepdims=True) + 1e-06)
    return (shaped * inverse_rms * gain_row).reshape(features.shape).astype(jnp.bfloat16)


def attend_heads(queries, key_rows, value_rows, query_ids, key_ids):
    row_count = queries.shape[0]
    key_count = key_rows.shape[0]
    pair_width = 2 * HEAD_DIM
    group_count = queries.shape[1] // pair_width
    score_scale = 2.0 / math.sqrt(HEAD_DIM)
    allowed = (key_ids[None, :] <= query_ids[:, None]) & (
        key_ids[None, :] >= query_ids[:, None] - 2
    )

    def pair_step(group_index, result):
        column = group_index * pair_width
        query_pair = lax.dynamic_slice_in_dim(queries, column, pair_width, 1).reshape(
            row_count, 2, HEAD_DIM
        )
        key_pair = lax.dynamic_slice_in_dim(key_rows, column, pair_width, 1).reshape(
            key_count, 2, HEAD_DIM
        )
        value_pair = lax.dynamic_slice_in_dim(value_rows, column, pair_width, 1).reshape(
            key_count, 2, HEAD_DIM
        )
        scores = (
            jnp.einsum("rhd,khd->hrk", query_pair, key_pair, preferred_element_type=jnp.float32)
            * score_scale
        )
        weights = jnp.where(allowed[None], jnp.exp(scores), 0.0)
        denominator = jnp.sum(weights, axis=-1)
        mixture = jnp.einsum(
            "hrk,khd->rhd",
            weights.astype(jnp.bfloat16),
            value_pair,
            preferred_element_type=jnp.float32,
        )
        mixture = mixture / jnp.transpose(denominator)[:, :, None]
        return lax.dynamic_update_slice_in_dim(
            result, mixture.reshape(row_count, pair_width), column, 1
        )

    initial = jnp.zeros((row_count, queries.shape[1]), jnp.float32)
    return lax.fori_loop(0, group_count, pair_step, initial)


def body(hidden_in, key_cache, value_cache, query_gain, key_gain, out_gate, span_ids):
    block_rows = hidden_in.shape[0]
    tm_index = lax.axis_index("tm")
    segment_index = lax.axis_index("segment")
    normed_keys = head_normalize(key_cache[0], key_gain[0])
    own_values = value_cache[0]
    first_row = tm_index * block_rows
    all_keys, all_values = (
        lax.all_gather(normed_keys, "tm", axis=0, tiled=True),
        lax.all_gather(own_values, "tm", axis=0, tiled=True),
    )

    def update(row_block):
        queries = head_normalize(row_block, query_gain[0])
        query_ids = lax.dynamic_slice_in_dim(span_ids, first_row, row_block.shape[0], 0)
        mixture = attend_heads(queries, all_keys, all_values, query_ids, span_ids)
        return (row_block.astype(jnp.float32) + out_gate[0] * mixture).astype(jnp.bfloat16)

    segments = lax.axis_size("segment")
    current = hidden_in
    result = hidden_in
    for section in range(segments):
        active = segment_index == section
        produced = lax.cond(active, lambda inputs: update(inputs), lambda inputs: inputs, current)
        result = jnp.where(active, produced, result)
        if section + 1 < segments:
            arrived = passed_along(produced, "segment", 1)
            current = jnp.where(segment_index == section + 1, arrived, current)
    return result[None]


def solution(mesh):
    placed = (
        P(("groups", "tm"), "head"),
        P("segment", ("groups", "tm"), "head"),
        P("segment", ("groups", "tm"), "head"),
        P("segment", None),
        P("segment", None),
        P("segment", "head"),
        P("groups"),
    )
    return jax.shard_map(
        body,
        mesh=mesh,
        in_specs=placed,
        out_specs=P("segment", ("groups", "tm"), "head"),
        check_vma=False,
    )
```

profile of v0, /device:TPU:2, one launch (start us, length us, event | category | flops | bytes accessed | tf_op | source)
XLA Modules:
  0.0 116.2 jit_solution(18251263530535177388)
XLA Ops:
  6.5 1.0 convert_multiply_fusion.4
  7.7 0.3 reduce_sum.53
  8.0 0.1 copy.59
  8.2 0.3 mul.154
  8.5 0.1 copy-done.2
  8.6 0.9 fusion.26
  9.6 0.7 all-gather.6.cloned.1.call-update
  10.4 30.9 %all-gather.4.cloned.1.call-done = bf16[384,1536]{1,0:T(8,128)(2,1)} async-done(((bf16[96,1536]{1,0:T(8,128)(2,1)}), bf16[384,1536]{1,0:T(8,128)(2,1)}) %all-gather.4.cloned.1.call-update) | async-done | bytes 1179664 | tf_op jit(solution)/shard_map/all_gather | solution.py:73
  41.2 31.1 %all-gather.6.cloned.1.call-done = bf16[1,384,1536]{2,1,0:T(8,128)(2,1)} async-done(((bf16[1,96,1536]{2,1,0:T(8,128)(2,1)}), bf16[1,384,1536]{2,1,0:T(8,128)(2,1)}) %all-gather.6.cloned.1.call-update) | async-done | bytes 1179664 | tf_op jit(solution)/shard_map/all_gather | solution.py:74
  72.4 1.3 %collective-permute-start = (bf16[96,1536]{1,0:T(8,128)(2,1)S(1)}, bf16[96,1536]{1,0:T(8,128)(2,1)S(1)}, u32[]{:S(2)}, u32[]{:S(2)}) collective-permute-start(bf16[96,1536]{1,0:T(8,128)(2,1)S(1)} %get-tuple-element.605), channel_id=1, source_target_pairs={{0,2},{1,3},{4,6},{5,7},{8,10},{9,11},{12,14},{13,15},{16,18},{17,... | collective-permute-start | bytes 884744 | tf_op jit(solution)/shard_map/ppermute | solution.py:13
  73.7 20.9 %collective-permute-done = bf16[96,1536]{1,0:T(8,128)(2,1)S(1)} collective-permute-done((bf16[96,1536]{1,0:T(8,128)(2,1)S(1)}, bf16[96,1536]{1,0:T(8,128)(2,1)S(1)}, u32[]{:S(2)}, u32[]{:S(2)}) %collective-permute-start) | collective-permute-done | bytes 294944 | tf_op jit(solution)/shard_map/ppermute | solution.py:13
  94.6 14.0 %conditional.3 = (bf16[96,1536]{1,0:T(8,128)(2,1)S(1)}) conditional(s32[]{:T(128)} %convert_element_type.58, bf16[96,1536]{1,0:T(8,128)(2,1)S(1)} %broadcast_select_fusion, (bf16[96,1536]{1,0:T(8,128)(2,1)S(1)}, f32[1,1536]{1,0:T(1,128)S(1)}, f32[1,128]{1,0:T(1,128)S(1)}, s32[384]{0:T(512)S(1)}, s32[]{:T(128)}, ...), branch_computations={%region_7.8_spmd, %region_8.13_spmd} | conditional | flops 39801896 | bytes 8945361 | solution.py:88
  94.8 0.3 reduce_sum.51
  95.3 0.3 mul.131
  95.6 0.2 fusion.22
  95.9 12.5 %while.27 = (s32[]{:T(128)}, f32[96,1536]{1,0:T(8,128)S(1)}, bf16[384,1536]{1,0:T(8,128)(2,1)}, bf16[96,1536]{1,0:T(8,128)(2,1)S(1)}, bf16[384,1536]{1,0:T(8,128...) while((s32[]{:T(128)}, f32[96,1536]{1,0:T(8,128)S(1)}, ...), condition=%wide.region_12.12_spmd.clone, body=%wide.region_10.11_spmd.clone.sunk | while | flops 38178628 | bytes 2682799 | solution.py:62
  95.9 1.1 constant_dynamic-slice_fusion.6
  97.0 0.2 copy.107
  97.3 0.3 fusion.48
  97.6 0.2 copy.106
  97.7 0.2 fusion.49
  98.0 1.1 constant_dynamic-slice_fusion.6
  99.1 0.2 copy.107
  99.3 0.3 fusion.48
  99.6 0.2 copy.106
  99.8 0.2 fusion.49
  100.1 1.1 constant_dynamic-slice_fusion.6
  101.1 0.2 copy.107
  101.4 0.3 fusion.48
  101.7 0.2 copy.106
  101.9 0.2 fusion.49
  102.2 1.1 constant_dynamic-slice_fusion.6
  103.2 0.2 copy.107
  103.5 0.3 fusion.48
  103.8 0.2 copy.106
  104.0 0.2 fusion.49
  104.3 1.1 constant_dynamic-slice_fusion.6
  105.3 0.2 copy.107
  105.6 0.3 fusion.48
  105.9 0.2 copy.106
  106.1 0.2 fusion.49
  106.3 1.1 constant_dynamic-slice_fusion.6
  107.4 0.2 copy.107
  107.7 0.3 fusion.48
  108.0 0.2 copy.106
  108.1 0.2 fusion.49
  108.4 0.2 fusion.23
  108.6 0.8 select_bitcast_fusion
  (42 shorter events, 1.6 us)
Async XLA Ops:
  6.5 1.6 %copy-start = (f32[1,128]{1,0:T(1,128)S(1)}, f32[1,128]{1,0:T(1,128)}, u32[]{:S(2)}) copy-start(f32[1,128]{1,0:T(1,128)} %param.19) | copy-start | bytes 1540
  6.5 34.7 %all-gather.4.cloned.1.call-start = ((), (), s32[]{:S(2)}) async-start(), calls=%async_computation | async-start | bytes 1474560 | tf_op jit(solution)/shard_map/all_gather | solution.py:73
  7.7 1.0 copy-start.2
  8.5 63.9 %copy-start.1 = (bf16[96,1536]{1,0:T(8,128)(2,1)S(1)}, bf16[96,1536]{1,0:T(8,128)(2,1)}, u32[]{:S(2)}) copy-start(bf16[96,1536]{1,0:T(8,128)(2,1)} %param.15) | copy-start | bytes 884740
  8.5 63.9 %copy-start.3 = (s32[384]{0:T(512)S(1)}, s32[384]{0:T(512)}, u32[]{:S(2)}) copy-start(s32[384]{0:T(512)} %param.21) | copy-start | bytes 4612
  8.5 63.9 %copy-start.4 = (f32[1,1536]{1,0:T(1,128)S(1)}, f32[1,1536]{1,0:T(1,128)}, u32[]{:S(2)}) copy-start(f32[1,1536]{1,0:T(1,128)} %param.20) | copy-start | bytes 18436
  8.5 63.9 %copy-start.5 = (f32[1,128]{1,0:T(1,128)S(1)}, f32[1,128]{1,0:T(1,128)}, u32[]{:S(2)}) copy-start(f32[1,128]{1,0:T(1,128)} %param.18) | copy-start | bytes 1540
  9.6 62.7 %all-gather.6.cloned.1.call-start = ((), (), s32[]{:S(2)}) async-start(), calls=%async_computation.1 | async-start | bytes 1474560 | tf_op jit(solution)/shard_map/all_gather | solution.py:74
  72.4 22.2 %collective-permute-start = (bf16[96,1536]{1,0:T(8,128)(2,1)S(1)}, bf16[96,1536]{1,0:T(8,128)(2,1)S(1)}, u32[]{:S(2)}, u32[]{:S(2)}) collective-permute-start(bf16[96,1536]{1,0:T(8,128)(2,1)S(1)} %get-tuple-element.605), channel_id=1, source_target_pairs={{0,2},{1,3},{4,6},{5,7},{8,10},{9,11},{12,14},{13,15},{16,18},{17,... | collective-permute-start | bytes 884744 | tf_op jit(solution)/shard_map/ppermute | solution.py:13
Sparse Core Ops, SparseCore 0:
  9.7 31.4 all-gather.3
  42.8 29.4 all-gather.5
where the time goes:
time: 116 us
  waiting for transfers between devices  83.5 us (72%)
  between operations  13.5 us (12%)
  local copies, waits for them, and re-layouts  9.74 us (8%)
  other arithmetic  4.47 us (4%)
  matrix products  3.17 us (3%)
  starting transfers between devices  1.34 us (1%)
    all_gather x1, waiting for transfers between devices, body(): lax.all_gather(own_values, 'tm', axis=0, tiled=True)  31.1 us
    all_gather x1, waiting for transfers between devices, body(): lax.all_gather(normed_keys, 'tm', axis=0, tiled=True)  30.9 us
    ppermute x1, waiting for transfers between devices, passed_along(): return lax.ppermute(shard, axis, pairs)  20.9 us
    dynamic_slice x12, local copies, waits for them, and re-layouts, pair_step(): lax.dynamic_slice_in_dim(key_rows, column, pair_width, 1)  7.31 us
  transfers between devices with their start and end apart: 3, of which 3 were waited for; matrix products, arithmetic and copies ran while one was open for 0% of the time, Pallas kernels for 0%

commit v1 on v0

--- a/solution.py
+++ b/solution.py
@@ -5,6 +5,11 @@
 from jax.sharding import PartitionSpec as P
 
 HEAD_DIM = 128
+
+
+def swapped_in(x, axis, dim):
+    stack = jnp.stack([x] * lax.axis_size(axis))
+    return jnp.concatenate(lax.all_to_all(stack, axis, 0, 0), axis=dim)
 
 
 def passed_along(shard, axis, by):
@@ -70,7 +75,7 @@
     own_values = value_cache[0]
     first_row = tm_index * block_rows
     all_keys, all_values = (
-        lax.all_gather(normed_keys, "tm", axis=0, tiled=True),
+        swapped_in(normed_keys, "tm", 0),
         lax.all_gather(own_values, "tm", axis=0, tiled=True),
     )
 

time: 116 us -> 112 us (0.966)
  waiting for transfers between devices: 83.5 us -> 68.8 us
  starting transfers between devices: 1.34 us -> 6.31 us
  other arithmetic: 4.47 us -> 8.28 us
    all_to_all x0 -> x1, waiting for transfers between devices: none -> 45.3 us  [swapped_in(): return jnp.concatenate(lax.all_to_all(stack, axis, 0, 0), axis=dim)]
    all_gather x1 -> x0, waiting for transfers between devices: 30.9 us -> none  [body(): lax.all_gather(normed_keys, 'tm', axis=0, tiled=True)]
    all_gather x1, waiting for transfers between devices: 31.1 us -> 1.78 us  [body(): lax.all_gather(own_values, 'tm', axis=0, tiled=True)]
    all_to_all x0 -> x1, starting transfers between devices: none -> 5.01 us  [swapped_in(): return jnp.concatenate(lax.all_to_all(stack, axis, 0, 0), axis=dim)]
    and x6, other arithmetic: 0.62 us -> 4.66 us  [attend_heads(): (key_ids[None, :] <= query_ids[:, None]) & (key_ids[None, :] >= query_ids...]
where the time goes in v1:
time: 112 us; the launch traced here: 111 us
  waiting for transfers between devices  68.8 us (61%)
  between operations  13.5 us (12%)
  local copies, waits for them, and re-layouts  10.6 us (9%)
  other arithmetic  8.28 us (7%)
  starting transfers between devices  6.31 us (6%)
  matrix products  3.18 us (3%)
    all_to_all x1, waiting for transfers between devices, swapped_in(): return jnp.concatenate(lax.all_to_all(stack, axis, 0, 0), axis=dim)  45.3 us
    ppermute x1, waiting for transfers between devices, passed_along(): return lax.ppermute(shard, axis, pairs)  21 us
    dynamic_slice x12, local copies, waits for them, and re-layouts, pair_step(): lax.dynamic_slice_in_dim(key_rows, column, pair_width, 1)  6.74 us
    all_to_all x1, starting transfers between devices, swapped_in(): return jnp.concatenate(lax.all_to_all(stack, axis, 0, 0), axis=dim)  5.01 us
    and x6, other arithmetic, attend_heads(): (key_ids[None, :] <= query_ids[:, None]) & (key_ids[None, :] >= query_ids...  4.66 us
  transfers between devices with their start and end apart: 3, of which 3 were waited for; matrix products, arithmetic and copies ran while one was open for 0% of the time, Pallas kernels for 0%

profile of v1, /device:TPU:2, one launch (start us, length us, event | category | flops | bytes accessed | tf_op | source)
XLA Modules:
  0.0 111.1 jit_solution(617120062675573460)
XLA Ops:
  6.5 1.0 convert_multiply_fusion.5
  7.7 0.3 reduce_sum.53
  8.2 0.3 mul.156
  8.6 0.4 copy-done.2
  9.0 1.1 %stack.10 = bf16[4,96,1536]{2,1,0:T(8,128)(2,1)} broadcast(bf16[96,1536]{1,0:T(8,128)(2,1)S(1)} %fusion.26), dimensions={1,2} | broadcast | bytes 1474560 | tf_op jit(solution)/shard_map/stack | solution.py:11
  10.1 5.0 %all-to-all-start = ((bf16[4,96,1536]{2,1,0:T(8,128)(2,1)}), bf16[4,96,1536]{2,1,0:T(8,128)(2,1)S(1)}, u32[]{:S(2)}, u32[]{:S(2)}) async-start(bf16[4,96,1536]{2,1,0:T(8,128)(2,1)} %stack.10), calls=%async_computation | async-start | bytes 2359296 | tf_op jit(solution)/shard_map/all_to_all | solution.py:12
  15.2 0.7 all-gather.3.cloned.1.call-update
  15.9 45.3 %all-to-all-done = bf16[4,96,1536]{2,1,0:T(8,128)(2,1)S(1)} async-done(((bf16[4,96,1536]{2,1,0:T(8,128)(2,1)}), bf16[4,96,1536]{2,1,0:T(8,128)(2,1)S(1)}, u32[]{:S(2)}, u32[]{:S(2)}) %all-to-all-start) | async-done | bytes 1179680 | tf_op jit(solution)/shard_map/all_to_all | solution.py:12
  61.2 1.8 %all-gather.3.cloned.1.call-done = bf16[1,384,1536]{2,1,0:T(8,128)(2,1)} async-done(((bf16[1,96,1536]{2,1,0:T(8,128)(2,1)}), bf16[1,384,1536]{2,1,0:T(8,128)(2,1)}) %all-gather.3.cloned.1.call-update) | async-done | bytes 1179664 | tf_op jit(solution)/shard_map/all_gather | solution.py:79
  63.1 1.3 %collective-permute-start = (bf16[96,1536]{1,0:T(8,128)(2,1)S(1)}, bf16[96,1536]{1,0:T(8,128)(2,1)S(1)}, u32[]{:S(2)}, u32[]{:S(2)}) collective-permute-start(bf16[96,1536]{1,0:T(8,128)(2,1)S(1)} %get-tuple-element.605), channel_id=1, source_target_pairs={{0,2},{1,3},{4,6},{5,7},{8,10},{9,11},{12,14},{13,15},{16,18},{17,... | collective-permute-start | bytes 884744 | tf_op jit(solution)/shard_map/ppermute | solution.py:18
  64.4 21.0 %collective-permute-done = bf16[96,1536]{1,0:T(8,128)(2,1)S(1)} collective-permute-done((bf16[96,1536]{1,0:T(8,128)(2,1)S(1)}, bf16[96,1536]{1,0:T(8,128)(2,1)S(1)}, u32[]{:S(2)}, u32[]{:S(2)}) %collective-permute-start) | collective-permute-done | bytes 294944 | tf_op jit(solution)/shard_map/ppermute | solution.py:18
  85.4 18.1 %conditional.3 = (bf16[96,1536]{1,0:T(8,128)(2,1)S(1)}) conditional(s32[]{:T(128)} %convert_element_type.55, bf16[96,1536]{1,0:T(8,128)(2,1)S(1)} %broadcast_select_fusion, (bf16[96,1536]{1,0:T(8,128)(2,1)S(1)}, f32[1,1536]{1,0:T(1,128)S(1)}, f32[1,128]{1,0:T(1,128)S(1)}, s32[384]{0:T(512)S(1)}, s32[]{:T(128)}, ...), branch_computations={%region_7.8_spmd, %region_8.13_spmd} | conditional | flops 39801896 | bytes 8945361 | solution.py:93
  85.4 0.7 broadcast_add_fusion.1
  86.3 0.3 reduce_sum.51
  86.8 0.3 mul.133
  87.0 0.2 fusion.22
  87.3 16.0 %while.27 = (s32[]{:T(128)}, f32[96,1536]{1,0:T(8,128)S(1)}, bf16[384,1536]{1,0:T(8,128)(2,1)}, bf16[96,1536]{1,0:T(8,128)(2,1)S(1)}, bf16[384,1536]{1,0:T(8,128...) while((s32[]{:T(128)}, f32[96,1536]{1,0:T(8,128)S(1)}, ...), condition=%wide.region_12.12_spmd.clone, body=%wide.region_10.11_spmd.clone.sunk | while | flops 38178628 | bytes 2682799 | solution.py:67
  87.3 1.0 constant_dynamic-slice_fusion.6
  88.5 0.8 compare_and_fusion.4
  89.3 0.3 fusion.48
  89.6 0.2 copy.114
  89.7 0.2 fusion.49
  90.0 1.0 constant_dynamic-slice_fusion.6
  91.1 0.8 compare_and_fusion.4
  91.9 0.3 fusion.48
  92.2 0.2 copy.114
  92.4 0.2 fusion.49
  92.7 1.0 constant_dynamic-slice_fusion.6
  93.8 0.8 compare_and_fusion.4
  94.6 0.3 fusion.48
  94.9 0.2 copy.114
  95.1 0.2 fusion.49
  95.3 1.0 constant_dynamic-slice_fusion.6
  96.5 0.8 compare_and_fusion.4
  97.2 0.3 fusion.48
  97.5 0.2 copy.114
  97.7 0.2 fusion.49
  98.0 1.0 constant_dynamic-slice_fusion.6
  99.1 0.8 compare_and_fusion.4
  99.9 0.3 fusion.48
  100.2 0.2 copy.114
  100.4 0.2 fusion.49
  100.6 1.0 constant_dynamic-slice_fusion.6
  101.8 0.8 compare_and_fusion.4
  102.6 0.3 fusion.48
  102.9 0.2 copy.114
  103.0 0.2 fusion.49
  103.5 0.8 select_bitcast_fusion
  (43 shorter events, 2.2 us)
Async XLA Ops:
  6.5 2.0 %copy-start = (f32[1,128]{1,0:T(1,128)S(1)}, f32[1,128]{1,0:T(1,128)}, u32[]{:S(2)}) copy-start(f32[1,128]{1,0:T(1,128)} %param.19) | copy-start | bytes 1540
  8.0 1.0 copy-start.2
  10.1 52.9 %copy-start.1 = (bf16[96,1536]{1,0:T(8,128)(2,1)S(1)}, bf16[96,1536]{1,0:T(8,128)(2,1)}, u32[]{:S(2)}) copy-start(bf16[96,1536]{1,0:T(8,128)(2,1)} %param.15) | copy-start | bytes 884740
  10.1 52.9 %copy-start.3 = (s32[384]{0:T(512)S(1)}, s32[384]{0:T(512)}, u32[]{:S(2)}) copy-start(s32[384]{0:T(512)} %param.21) | copy-start | bytes 4612
  10.1 52.9 %copy-start.4 = (f32[1,1536]{1,0:T(1,128)S(1)}, f32[1,1536]{1,0:T(1,128)}, u32[]{:S(2)}) copy-start(f32[1,1536]{1,0:T(1,128)} %param.20) | copy-start | bytes 18436
  10.1 52.9 %copy-start.5 = (f32[1,128]{1,0:T(1,128)S(1)}, f32[1,128]{1,0:T(1,128)}, u32[]{:S(2)}) copy-start(f32[1,128]{1,0:T(1,128)} %param.18) | copy-start | bytes 1540
  10.1 51.1 %all-to-all-start = ((bf16[4,96,1536]{2,1,0:T(8,128)(2,1)}), bf16[4,96,1536]{2,1,0:T(8,128)(2,1)S(1)}, u32[]{:S(2)}, u32[]{:S(2)}) async-start(bf16[4,96,1536]{2,1,0:T(8,128)(2,1)} %stack.10), calls=%async_computation | async-start | bytes 2359296 | tf_op jit(solution)/shard_map/all_to_all | solution.py:12
  15.2 47.8 %all-gather.3.cloned.1.call-start = ((), (), s32[]{:S(2)}) async-start(), calls=%async_computation.1 | async-start | bytes 1474560 | tf_op jit(solution)/shard_map/all_gather | solution.py:79
  63.1 22.3 %collective-permute-start = (bf16[96,1536]{1,0:T(8,128)(2,1)S(1)}, bf16[96,1536]{1,0:T(8,128)(2,1)S(1)}, u32[]{:S(2)}, u32[]{:S(2)}) collective-permute-start(bf16[96,1536]{1,0:T(8,128)(2,1)S(1)} %get-tuple-element.605), channel_id=1, source_target_pairs={{0,2},{1,3},{4,6},{5,7},{8,10},{9,11},{12,14},{13,15},{16,18},{17,... | collective-permute-start | bytes 884744 | tf_op jit(solution)/shard_map/ppermute | solution.py:18
Sparse Core Ops, SparseCore 0:
  17.5 45.4 all-gather.2
